TPU v7x, 256 devices: a whole 4x4x8 slice. The times are simulated.
256 devices in a mesh: aux: 32 (over z, x), occ: 8 (over y, core).
Axes of the slice: x: 4, y: 4, z: 8, core: 2. Of those that a mesh axis runs over, the one named last changes fastest.
Arguments:
- half_integrals: float32 [2048, 256, 768], P('aux', 'occ'), may hold values from -2 to 2
- virtual_orbitals: float32 [768, 512], replicated, may hold values from -0.21875 to 0.21875
- occupied_energy: float32 [256], replicated, may hold values from -2 to -0.3
- virtual_energy: float32 [512], replicated, may hold values from 0.3 to 3
- partners: int32 [256, 1], replicated, may hold values from 0 to 255, as said below
Outputs:
- density: float32 [2048, 256, 512], P('aux', 'occ')
Inputs may be any that keep to these rules, and one draw needn't show every extreme that they name: `partners`: occupied orbitals form 8 groups of 32 consecutive ones; of the 32 entries of one group, at most 6 lie in any one group, and exactly 6 in some group.
All inputs are finite; a program needn't handle non-finite values.
Results may differ from a plain program's by a relative error of at most 0.00007.
Values sent between devices are 32-bit elements; how exact they have to be, the bound alone decides.
A program may use at most 128 MiB of HBM per device.

v0:
```python
import jax
import jax.numpy as jnp
from jax import lax
from jax.sharding import PartitionSpec as P


def split_up(array, dim, devices):
    before, after = (array.shape[:dim], array.shape[dim + 1 :])
    return jnp.moveaxis(array.reshape(*before, devices, -1, *after), dim, 0)


def piece_ends(length, count):
    turn = length // count
    if turn >= 8:
        turn -= turn % 8
    return [turn * k for k in range(1, count)]


def in_order(blocks, dim):
    blocks = jnp.moveaxis(blocks, 0, dim)
    lengths = blocks.shape
    return blocks.reshape(*lengths[:dim], lengths[dim] * lengths[dim + 1], *lengths[dim + 2 :])


def exchange_in_pieces(array, axis, pieces, split_dim, concat_dim):
    blocks = split_up(array, split_dim, lax.axis_size(axis))
    split_at = max(range(1, max(2, blocks.ndim - 1)), key=lambda d: blocks.shape[d])
    finished = []
    for share in jnp.split(blocks, piece_ends(blocks.shape[split_at], pieces), axis=split_at):
        if share.size:
            finished.append(lax.all_to_all(share, axis, split_axis=0, concat_axis=0, tiled=True))
    return in_order(jnp.concatenate(finished, axis=split_at), concat_dim)


def local(half_integrals, virtual_orbitals, occupied_energy, virtual_energy, partners):
    highest = lax.Precision.HIGHEST
    groups = lax.axis_size("occ")
    my_group = lax.axis_index("occ")
    my_column = lax.axis_index("aux")
    group_size = half_integrals.shape[1]
    pair_count = partners.shape[1]
    requests = group_size * pair_count
    capacity = requests // groups + 2
    working = jnp.einsum("qim,mv->qiv", half_integrals, virtual_orbitals, precision=highest)
    row_width = working.shape[2]
    slices = working.shape[0]
    source_group = (partners // group_size).reshape(groups, requests)
    local_index = (partners % group_size).reshape(groups, requests)
    request_ids = jnp.arange(requests, dtype=jnp.int32)
    earlier = request_ids[:, None] > request_ids[None, :]
    same_source = source_group[:, :, None] == source_group[:, None, :]
    slot_rank = jnp.sum((same_source & earlier[None]).astype(jnp.int32), axis=2)
    outgoing = (source_group == my_group).astype(jnp.int32)
    slot_ids = jnp.arange(capacity, dtype=jnp.int32)
    slot_match = outgoing[:, None, :] * (slot_rank[:, None, :] == slot_ids[None, :, None]).astype(
        jnp.int32
    )
    chosen = jnp.sum(slot_match * local_index[:, None, :], axis=2).reshape(-1)
    filled = jnp.sum(slot_match, axis=2).reshape(-1)
    outbound = jnp.take(working, chosen, axis=1) * filled.astype(working.dtype)[None, :, None]
    outbound = outbound.reshape(slices, groups, capacity, row_width)
    inbound = lax.all_to_all(outbound, "occ", split_axis=1, concat_axis=1, tiled=True)
    my_sources = lax.dynamic_index_in_dim(source_group, my_group, 0, keepdims=False)
    my_ranks = lax.dynamic_index_in_dim(slot_rank, my_group, 0, keepdims=False)
    partner_rows = jnp.take(
        inbound.reshape(slices, groups * capacity, row_width),
        my_sources * capacity + my_ranks,
        axis=1,
    )
    partner_rows = partner_rows.reshape(slices, group_size, pair_count, row_width)
    per_device = group_size // lax.axis_size("aux")
    first_orbital = my_group * group_size + my_column * per_device
    own_energy = lax.dynamic_slice_in_dim(occupied_energy, first_orbital, per_device, 0)
    own_partners = lax.dynamic_slice_in_dim(partners, first_orbital, per_device, 0)
    orbital_ids = jnp.arange(occupied_energy.shape[0], dtype=jnp.int32)
    partner_energy = jnp.sum(
        jnp.where(
            own_partners[:, :, None] == orbital_ids[None, None, :],
            occupied_energy[None, None, :],
            jnp.float32(0.0),
        ),
        axis=2,
    )
    pair_energy = (
        jnp.concatenate([own_energy[:, None], partner_energy], axis=1) + own_energy[:, None]
    )
    denominator = (
        virtual_energy[None, None, :, None]
        + virtual_energy[None, None, None, :]
        - pair_energy[:, :, None, None]
    )
    own_rows = exchange_in_pieces(working, "aux", 2, 1, 0)
    self_ints = jnp.einsum("qda,qdb->dab", own_rows, own_rows, precision=highest)
    self_amplitude = self_ints / denominator[:, 0]
    self_term = jnp.einsum("dab,qdb->qda", self_amplitude, own_rows, precision=highest)
    member_rows = lax.all_to_all(partner_rows, "aux", split_axis=1, concat_axis=0, tiled=True)
    cross_ints = jnp.einsum("qda,qdkb->dkab", own_rows, member_rows, precision=highest)
    cross_amplitude = cross_ints / denominator[:, 1:]
    gathered = self_term + jnp.einsum(
        "dkab,qdkb->qda", cross_amplitude, member_rows, precision=highest
    )
    return lax.all_to_all(gathered, "aux", split_axis=0, concat_axis=1, tiled=True)


def solution(mesh):
    return jax.shard_map(
        local,
        mesh=mesh,
        in_specs=(P("aux", "occ", None), P(), P(), P(), P()),
        out_specs=P("aux", "occ", None),
        check_vma=False,
    )
```

profile of v0, /device:TPU:2, one launch (start us, length us, event | category | flops | bytes accessed | tf_op | source)
XLA Modules:
  0.0 455.3 jit_solution(16977519400593986430)
XLA Ops:
  1.4 12.3 %fusion.3 = f32[64,32,512]{2,1,0:T(8,128)S(1)} fusion(f32[64,32,768]{2,1,0:T(8,128)} %param.5, f32[768,512]{1,0:T(8,128)S(1)} %copy-done), kind=kOutput, calls=%fused_computation.11 | convolution fusion | flops 9663676416 | bytes 12058624 | tf_op jit(solution)/shard_map/qim,mv->qiv/dot_general | solution.py:44
  18.9 11.7 %all-to-all-start = ((f32[32,32,1,512]{3,1,2,0:T(8,128)}), f32[32,32,1,512]{3,1,2,0:T(8,128)}, u32[]{:S(2)}, u32[]{:S(2)}) async-start(f32[32,32,1,512]{3,1,2,0:T(8,128)} %copy.20), calls=%async_computation | async-start | bytes 4194304 | tf_op jit(solution)/shard_map/all_to_all | solution.py:31
  30.6 6.6 %copy.27 = f32[64,32,512]{2,0,1:T(8,128)} copy(f32[64,32,512]{2,1,0:T(8,128)} %copy-done.3) | data formatting | bytes 8388608 | tf_op jit(solution)/shard_map/qim,mv->qiv/dot_general | solution.py:44
  38.4 5.8 %gather_fusion = f32[48,64,512]{2,1,0:T(8,128)} fusion(f32[64,32,512]{2,0,1:T(8,128)} %copy.27, s32[1024]{0:T(1024)S(1)} %pad_clamp_fusion.1), kind=kCustom, calls=%fused_computation | custom fusion | bytes 12583104 | tf_op jit(solution)/shard_map/jit(_take)/gather | solution.py:60
  44.2 6.9 %select_multiply_fusion = f32[64,8,6,512]{3,0,2,1:T(8,128)} fusion(f32[64,8,6,512]{3,0,2,1:T(8,128)} %bitcast.78, f32[8,6]{1,0:T(8,128)S(1)} %copy.28, pred[8,6]{1,0:T(8,128)(4,1)S(1)} %copy.25), kind=kLoop, calls=%fused_computation.2 | loop fusion | flops 3145728 | bytes 12583152 | tf_op jit(solution)/shard_map/mul | solution.py:60
  51.1 28.8 %all-to-all-done = f32[32,32,1,512]{3,1,2,0:T(8,128)} async-done(((f32[32,32,1,512]{3,1,2,0:T(8,128)}), f32[32,32,1,512]{3,1,2,0:T(8,128)}, u32[]{:S(2)}, u32[]{:S(2)}) %all-to-all-start) | async-done | bytes 2097184 | tf_op jit(solution)/shard_map/all_to_all | solution.py:31
  79.9 15.5 %all-to-all-start.2 = ((f32[64,8,6,512]{3,0,2,1:T(8,128)}), f32[64,8,6,512]{3,0,2,1:T(8,128)}, u32[]{:S(2)}, u32[]{:S(2)}) async-start(f32[64,8,6,512]{3,0,2,1:T(8,128)} %select_multiply_fusion), calls=%async_computation.2 | async-start | bytes 12582912 | tf_op jit(solution)/shard_map/all_to_all | solution.py:62
  95.4 4.1 copy.21
  99.5 68.0 %all-to-all-done.2 = f32[64,8,6,512]{3,0,2,1:T(8,128)} async-done(((f32[64,8,6,512]{3,0,2,1:T(8,128)}), f32[64,8,6,512]{3,0,2,1:T(8,128)}, u32[]{:S(2)}, u32[]{:S(2)}) %all-to-all-start.2) | async-done | bytes 6291488 | tf_op jit(solution)/shard_map/all_to_all | solution.py:62
  167.5 6.9 %all-to-all-start.1 = ((f32[32,32,1,512]{3,1,2,0:T(8,128)}), f32[32,32,1,512]{3,1,2,0:T(8,128)}, u32[]{:S(2)}, u32[]{:S(2)}) async-start(f32[32,32,1,512]{3,1,2,0:T(8,128)} %copy.21), calls=%async_computation.1 | async-start | bytes 4194304 | tf_op jit(solution)/shard_map/all_to_all | solution.py:31
  174.5 5.6 %gather_fusion.1 = f32[32,64,512]{2,1,0:T(8,128)} fusion(f32[64,48,512]{2,0,1:T(8,128)} %bitcast.15, s32[1024]{0:T(1024)S(1)} %pad_clamp_fusion), kind=kCustom, calls=%fused_computation.1 | custom fusion | bytes 8388736 | tf_op jit(solution)/shard_map/jit(_take)/gather | solution.py:65
  180.1 5.0 %fusion = f32[64,32,1,512]{3,0,2,1:T(8,128)} fusion(f32[32,64,512]{2,1,0:T(8,128)} %gather_fusion.1, pred[32]{0:T(512)(128)(4,1)S(1)} %get-tuple-element.9), kind=kLoop, calls=%fused_computation.4 | loop fusion | flops 1048576 | bytes 8388640 | tf_op jit(solution)/shard_map/jit(_take)/select_n | solution.py:65
  185.1 38.5 %all-to-all-done.1 = f32[32,32,1,512]{3,1,2,0:T(8,128)} async-done(((f32[32,32,1,512]{3,1,2,0:T(8,128)}), f32[32,32,1,512]{3,1,2,0:T(8,128)}, u32[]{:S(2)}, u32[]{:S(2)}) %all-to-all-start.1) | async-done | bytes 2097184 | tf_op jit(solution)/shard_map/all_to_all | solution.py:31
  223.6 6.9 %all-to-all-start.3 = ((f32[64,32,1,512]{3,0,2,1:T(8,128)}), f32[64,32,1,512]{3,0,2,1:T(8,128)}, u32[]{:S(2)}, u32[]{:S(2)}) async-start(f32[64,32,1,512]{3,0,2,1:T(8,128)} %fusion), calls=%async_computation.3 | async-start | bytes 8388608 | tf_op jit(solution)/shard_map/all_to_all | solution.py:96
  235.4 3.6 copy_dynamic-update-slice_fusion.1
  238.9 2.8 copy_dynamic-update-slice_fusion
  244.2 7.0 %fusion.8 = f32[512,512]{1,0:T(8,128)S(1)} fusion(f32[32,64,1,512]{3,0,1,2:T(8,128)S(1)} %copy_dynamic-update-slice_fusion, f32[1,2,512,512]{3,2,1,0:T(8,128)S(1)} %broadcast_subtract_fusion), kind=kOutput, calls=%fused_computation.15 | convolution fusion | flops 6442713088 | bytes 6291456 | tf_op jit(solution)/shard_map/qda,qdb->dab/dot_general | solution.py:93
  251.2 8.3 %fusion.23 = f32[2048,512]{1,0:T(8,128)} fusion(f32[2048,512]{1,0:T(8,128)S(1)} %bitcast.75, f32[512,512]{1,0:T(8,128)S(1)} %fusion.8), kind=kOutput, calls=%fused_computation.54 | convolution fusion | flops 6442450944 | bytes 9437184 | tf_op jit(solution)/shard_map/dab,qdb->qda/dot_general | solution.py:95
  259.5 63.2 %all-to-all-done.3 = f32[64,32,1,512]{3,0,2,1:T(8,128)} async-done(((f32[64,32,1,512]{3,0,2,1:T(8,128)}), f32[64,32,1,512]{3,0,2,1:T(8,128)}, u32[]{:S(2)}, u32[]{:S(2)}) %all-to-all-start.3) | async-done | bytes 4194336 | tf_op jit(solution)/shard_map/all_to_all | solution.py:96
  322.7 9.9 %fusion.12 = f32[512,512]{1,0:T(8,128)S(1)} fusion(f32[2048,512]{1,0:T(8,128)} %bitcast.23, f32[2048,512]{1,0:T(8,128)} %bitcast.76, f32[1,2,512,512]{3,2,1,0:T(8,128)} %copy-done.5), kind=kOutput, calls=%fused_computation.17 | convolution fusion | flops 6442713088 | bytes 10485760 | tf_op jit(solution)/shard_map/qda,qdkb->dkab/dot_general | solution.py:97
  332.6 8.6 %add_bitcast_fusion = f32[2048,1,512]{2,0,1:T(8,128)S(1)} fusion(f32[2048,512]{1,0:T(8,128)S(1)} %copy-done.4, f32[2048,512]{1,0:T(8,128)} %bitcast.23, f32[512,512]{1,0:T(8,128)S(1)} %fusion.12), kind=kOutput, calls=%fused_computation.8 | convolution fusion | flops 6443499520 | bytes 13631488 | tf_op jit(solution)/shard_map/dkab,qdkb->qda/dot_general | solution.py:99
  341.2 8.0 %copy.31 = f32[2048,1,512]{2,1,0:T(1,128)S(1)} copy(f32[2048,1,512]{2,0,1:T(8,128)S(1)} %add_bitcast_fusion) | data formatting | bytes 8388608 | tf_op jit(solution)/shard_map/add | solution.py:99
  349.2 101.2 %all_to_all.48 = f32[2048,1,512]{2,1,0:T(1,128)S(1)} all-to-all(f32[2048,1,512]{2,1,0:T(1,128)S(1)} %copy.31), channel_id=1, replica_groups=mesh['aux'=32,'occ'=8] {'aux'}, dimensions={0} | all-to-all | bytes 8388608 | tf_op jit(solution)/shard_map/all_to_all | solution.py:102
  450.4 4.4 copy.37
  (45 shorter events, 15.1 us)
Async XLA Ops:
  0.0 1.4 copy-start
  13.7 2.7 copy-start.3
  18.9 61.0 %all-to-all-start = ((f32[32,32,1,512]{3,1,2,0:T(8,128)}), f32[32,32,1,512]{3,1,2,0:T(8,128)}, u32[]{:S(2)}, u32[]{:S(2)}) async-start(f32[32,32,1,512]{3,1,2,0:T(8,128)} %copy.20), calls=%async_computation | async-start | bytes 4194304 | tf_op jit(solution)/shard_map/all_to_all | solution.py:31
  30.6 6.6 %copy-start.7 = (s32[256,1]{0,1:T(1,128)S(1)}, s32[256,1]{0,1:T(1,128)}, u32[]{:S(2)}) copy-start(s32[256,1]{0,1:T(1,128)} %param.9) | copy-start | bytes 3076
  79.9 87.6 %all-to-all-start.2 = ((f32[64,8,6,512]{3,0,2,1:T(8,128)}), f32[64,8,6,512]{3,0,2,1:T(8,128)}, u32[]{:S(2)}, u32[]{:S(2)}) async-start(f32[64,8,6,512]{3,0,2,1:T(8,128)} %select_multiply_fusion), calls=%async_computation.2 | async-start | bytes 12582912 | tf_op jit(solution)/shard_map/all_to_all | solution.py:62
  167.5 56.0 %all-to-all-start.1 = ((f32[32,32,1,512]{3,1,2,0:T(8,128)}), f32[32,32,1,512]{3,1,2,0:T(8,128)}, u32[]{:S(2)}, u32[]{:S(2)}) async-start(f32[32,32,1,512]{3,1,2,0:T(8,128)} %copy.21), calls=%async_computation.1 | async-start | bytes 4194304 | tf_op jit(solution)/shard_map/all_to_all | solution.py:31
  185.1 46.0 %copy-start.8 = (f32[256]{0:T(256)S(1)}, f32[256]{0:T(256)}, u32[]{:S(2)}) copy-start(f32[256]{0:T(256)} %param.7) | copy-start | bytes 3076
  185.1 49.8 %copy-start.6 = (f32[512]{0:T(512)S(1)}, f32[512]{0:T(512)}, u32[]{:S(2)}) copy-start(f32[512]{0:T(512)} %param.8) | copy-start | bytes 6148
  223.6 99.2 %all-to-all-start.3 = ((f32[64,32,1,512]{3,0,2,1:T(8,128)}), f32[64,32,1,512]{3,0,2,1:T(8,128)}, u32[]{:S(2)}, u32[]{:S(2)}) async-start(f32[64,32,1,512]{3,0,2,1:T(8,128)} %fusion), calls=%async_computation.3 | async-start | bytes 8388608 | tf_op jit(solution)/shard_map/all_to_all | solution.py:96
  235.4 8.8 %copy-start.5 = (f32[1,2,512,512]{3,2,1,0:T(8,128)}, f32[1,2,512,512]{3,2,1,0:T(8,128)S(1)}, u32[]{:S(2)}) copy-start(f32[1,2,512,512]{3,2,1,0:T(8,128)S(1)} %broadcast_subtract_fusion) | copy-start | bytes 6291460
  244.2 7.0 %copy-start.2 = (f32[32,64,1,512]{3,1,0,2:T(8,128)}, f32[32,64,1,512]{3,1,0,2:T(8,128)S(1)}, u32[]{:S(2)}) copy-start(f32[32,64,1,512]{3,1,0,2:T(8,128)S(1)} %copy.24) | copy-start | bytes 12582916
  322.7 9.9 %copy-start.4 = (f32[2048,512]{1,0:T(8,128)S(1)}, f32[2048,512]{1,0:T(8,128)}, u32[]{:S(2)}) copy-start(f32[2048,512]{1,0:T(8,128)} %fusion.23) | copy-start | bytes 12582916
  450.4 4.4 copy-start.1
where the time goes:
time: 464 us; the launch traced here: 455 us
  waiting for transfers between devices  199 us (43%)
  blocking collectives  101 us (22%)
  local copies, waits for them, and re-layouts  51.8 us (11%)
  matrix products  46 us (10%)
  starting transfers between devices  40.9 us (9%)
  other arithmetic  16.2 us (3%)
    all_to_all x1, blocking collectives, local(): lax.all_to_all(gathered, 'aux', split_axis=0, concat_axis=1, tiled=True)  101 us
    all_to_all x1, waiting for transfers between devices, local(): lax.all_to_all(outbound, 'occ', split_axis=1, concat_axis=1, tiled=True)  68 us
    all_to_all x2, waiting for transfers between devices, exchange_in_pieces(): lax.all_to_all(share, axis, split_axis=0, concat_axis=0, tiled=True)  67.3 us
    all_to_all x1, waiting for transfers between devices, local(): lax.all_to_all(partner_rows, 'aux', split_axis=1, concat_axis=0, tiled=True)  63.2 us
    all_to_all x2, starting transfers between devices, exchange_in_pieces(): lax.all_to_all(share, axis, split_axis=0, concat_axis=0, tiled=True)  18.6 us
    all_to_all x1, starting transfers between devices, local(): lax.all_to_all(outbound, 'occ', split_axis=1, concat_axis=1, tiled=True)  15.5 us
    dot_general x1, matrix products, local(): jnp.einsum('qim,mv->qiv', half_integrals, virtual_orbitals, precision=hig...  12.3 us
    dot_general x1, matrix products, local(): jnp.einsum('qda,qdkb->dkab', own_rows, member_rows, precision=highest)  9.86 us
  transfers between devices with their start and end apart: 4, of which 4 were waited for; matrix products, arithmetic and copies ran while one was open for 14% of the time, Pallas kernels for 0%

commit v1 on v0

--- a/solution.py
+++ b/solution.py
@@ -2,6 +2,18 @@
 import jax.numpy as jnp
 from jax import lax
 from jax.sharding import PartitionSpec as P
+
+
+def split_up_2(shard, dim, devices):
+    dims = shard.shape
+    blocks = shard.reshape(*dims[:dim], devices, dims[dim] // devices, *dims[dim + 1 :])
+    return jnp.moveaxis(blocks, dim, 0)
+
+
+def laid_out(pieces, dim):
+    pieces = jnp.moveaxis(pieces, 0, dim)
+    shape = pieces.shape
+    return pieces.reshape(*shape[:dim], shape[dim] * shape[dim + 1], *shape[dim + 2 :])
 
 
 def split_up(array, dim, devices):
@@ -59,7 +71,14 @@
     filled = jnp.sum(slot_match, axis=2).reshape(-1)
     outbound = jnp.take(working, chosen, axis=1) * filled.astype(working.dtype)[None, :, None]
     outbound = outbound.reshape(slices, groups, capacity, row_width)
-    inbound = lax.all_to_all(outbound, "occ", split_axis=1, concat_axis=1, tiled=True)
+    size, mine = (lax.axis_size("occ"), lax.axis_index("occ"))
+    blocks_2 = split_up_2(outbound, 1, size)
+    outs = [blocks_2[mine]]
+    for step in range(1, size):
+        sent = blocks_2[mine ^ step]
+        outs.append(lax.ppermute(sent, "occ", [(i, i ^ step) for i in range(size)]))
+    blocks_2 = jnp.stack(outs)[mine ^ jnp.arange(size)]
+    inbound = laid_out(blocks_2, 1)
     my_sources = lax.dynamic_index_in_dim(source_group, my_group, 0, keepdims=False)
     my_ranks = lax.dynamic_index_in_dim(slot_rank, my_group, 0, keepdims=False)
     partner_rows = jnp.take(

time: 464 us -> 447 us (0.963)
  waiting for transfers between devices: 199 us -> 173 us
  local copies, waits for them, and re-layouts: 51.8 us -> 66.5 us
    all_to_all x1 -> x0, waiting for transfers between devices: 68 us -> none  [local(): lax.all_to_all(outbound, 'occ', split_axis=1, concat_axis=1, tiled=True)]
    ppermute x0 -> x7, waiting for transfers between devices: none -> 60.7 us  [local(): outs.append(lax.ppermute(sent, 'occ', [(i, i ^ step) for i in range(size)]))]
    all_to_all x2, waiting for transfers between devices: 67.3 us -> 44.1 us  [exchange_in_pieces(): lax.all_to_all(share, axis, split_axis=0, concat_axis=0, tiled=True)]
    all_to_all x1 -> x0, starting transfers between devices: 15.5 us -> none  [local(): lax.all_to_all(outbound, 'occ', split_axis=1, concat_axis=1, tiled=True)]
    ppermute x0 -> x7, starting transfers between devices: none -> 10.1 us  [local(): outs.append(lax.ppermute(sent, 'occ', [(i, i ^ step) for i in range(size)]))]
    unnamed x19 -> x26, local copies, waits for them, and re-layouts: 5.35 us -> 12.1 us
    gather x0 -> x1, local copies, waits for them, and re-layouts: none -> 6.39 us  [local(): blocks_2 = jnp.stack(outs)[mine ^ jnp.arange(size)]]
    all_to_all x1, waiting for transfers between devices: 63.2 us -> 68.4 us  [local(): lax.all_to_all(partner_rows, 'aux', split_axis=1, concat_axis=0, tiled=True)]
  transfers between devices with their start and end apart: 4 -> 10, of which waited for: 4 -> 7; matrix products, arithmetic and copies ran while one was open for 14% -> 17% of each run, Pallas kernels for 0% -> 0%
where the time goes in v1:
time: 447 us; the launch traced here: 439 us
  waiting for transfers between devices  173 us (39%)
  blocking collectives  100 us (22%)
  local copies, waits for them, and re-layouts  66.5 us (15%)
  matrix products  46 us (10%)
  starting transfers between devices  39.5 us (9%)
  other arithmetic  13.3 us (3%)
    all_to_all x1, blocking collectives, local(): lax.all_to_all(gathered, 'aux', split_axis=0, concat_axis=1, tiled=True)  100 us
    all_to_all x1, waiting for transfers between devices, local(): lax.all_to_all(partner_rows, 'aux', split_axis=1, concat_axis=0, tiled=True)  68.4 us
    ppermute x7, waiting for transfers between devices, local(): outs.append(lax.ppermute(sent, 'occ', [(i, i ^ step) for i in range(size)]))  60.7 us
    all_to_all x2, waiting for transfers between devices, exchange_in_pieces(): lax.all_to_all(share, axis, split_axis=0, concat_axis=0, tiled=True)  44.1 us
    all_to_all x2, starting transfers between devices, exchange_in_pieces(): lax.all_to_all(share, axis, split_axis=0, concat_axis=0, tiled=True)  19.3 us
    dot_general x1, matrix products, local(): jnp.einsum('qim,mv->qiv', half_integrals, virtual_orbitals, precision=hig...  12.3 us
    unnamed x26, local copies, waits for them, and re-layouts  12.1 us
    all_to_all x1, starting transfers between devices, local(): lax.all_to_all(partner_rows, 'aux', split_axis=1, concat_axis=0, tiled=True)  10.1 us
  transfers between devices with their start and end apart: 10, of which 7 were waited for; matrix products, arithmetic and copies ran while one was open for 17% of the time, Pallas kernels for 0%

profile of v1, /device:TPU:2, one launch (start us, length us, event | category | flops | bytes accessed | tf_op | source)
XLA Modules:
  0.0 439.2 jit_solution(4263117590002673382)
XLA Ops:
  1.4 12.3 %fusion.3 = f32[64,32,512]{2,1,0:T(8,128)S(1)} fusion(f32[64,32,768]{2,1,0:T(8,128)} %param.5, f32[768,512]{1,0:T(8,128)S(1)} %copy-done), kind=kOutput, calls=%fused_computation.12 | convolution fusion | flops 9663676416 | bytes 12058624 | tf_op jit(solution)/shard_map/qim,mv->qiv/dot_general | solution.py:56
  18.9 11.7 %all-to-all-start = ((f32[32,32,1,512]{3,1,2,0:T(8,128)}), f32[32,32,1,512]{3,1,2,0:T(8,128)}, u32[]{:S(2)}, u32[]{:S(2)}) async-start(f32[32,32,1,512]{3,1,2,0:T(8,128)} %copy.20), calls=%async_computation | async-start | bytes 4194304 | tf_op jit(solution)/shard_map/all_to_all | solution.py:43
  31.6 4.2 copy.21
  35.8 44.1 %all-to-all-done = f32[32,32,1,512]{3,1,2,0:T(8,128)} async-done(((f32[32,32,1,512]{3,1,2,0:T(8,128)}), f32[32,32,1,512]{3,1,2,0:T(8,128)}, u32[]{:S(2)}, u32[]{:S(2)}) %all-to-all-start) | async-done | bytes 2097184 | tf_op jit(solution)/shard_map/all_to_all | solution.py:43
  79.9 7.6 %all-to-all-start.1 = ((f32[32,32,1,512]{3,1,2,0:T(8,128)}), f32[32,32,1,512]{3,1,2,0:T(8,128)}, u32[]{:S(2)}, u32[]{:S(2)}) async-start(f32[32,32,1,512]{3,1,2,0:T(8,128)} %copy.21), calls=%async_computation.1 | async-start | bytes 4194304 | tf_op jit(solution)/shard_map/all_to_all | solution.py:43
  87.6 6.6 %copy.27 = f32[64,32,512]{2,0,1:T(8,128)} copy(f32[64,32,512]{2,1,0:T(8,128)} %copy-done.3) | data formatting | bytes 8388608 | tf_op jit(solution)/shard_map/qim,mv->qiv/dot_general | solution.py:56
  94.4 5.8 %gather_fusion = f32[48,64,512]{2,1,0:T(8,128)} fusion(f32[64,32,512]{2,0,1:T(8,128)} %copy.27, s32[1024]{0:T(1024)S(1)} %get-tuple-element.21), kind=kCustom, calls=%fused_computation | custom fusion | bytes 12583104 | tf_op jit(solution)/shard_map/jit(_take)/gather | solution.py:72
  100.2 4.1 select_multiply_fusion
  115.1 10.4 %collective-permute-done.1 = f32[64,1,6,512]{3,0,2,1:T(8,128)S(1)} collective-permute-done((f32[64,1,6,512]{3,0,2,1:T(8,128)S(1)}, f32[64,1,6,512]{3,0,2,1:T(8,128)S(1)}, u32[]{:S(2)}, u32[]{:S(2)}) %collective-permute-start.1) | collective-permute-done | bytes 786464 | tf_op jit(solution)/shard_map/ppermute | solution.py:79
  128.2 13.1 %collective-permute-done.2 = f32[64,1,6,512]{3,0,2,1:T(8,128)S(1)} collective-permute-done((f32[64,1,6,512]{3,0,2,1:T(8,128)S(1)}, f32[64,1,6,512]{3,0,2,1:T(8,128)S(1)}, u32[]{:S(2)}, u32[]{:S(2)}) %collective-permute-start.2) | collective-permute-done | bytes 786464 | tf_op jit(solution)/shard_map/ppermute | solution.py:79
  142.3 19.4 %collective-permute-done.3 = f32[64,1,6,512]{3,0,2,1:T(8,128)S(1)} collective-permute-done((f32[64,1,6,512]{3,0,2,1:T(8,128)S(1)}, f32[64,1,6,512]{3,0,2,1:T(8,128)S(1)}, u32[]{:S(2)}, u32[]{:S(2)}) %collective-permute-start.3) | collective-permute-done | bytes 786464 | tf_op jit(solution)/shard_map/ppermute | solution.py:79
  162.6 15.0 %collective-permute-done.4 = f32[64,1,6,512]{3,0,2,1:T(8,128)S(1)} collective-permute-done((f32[64,1,6,512]{3,0,2,1:T(8,128)S(1)}, f32[64,1,6,512]{3,0,2,1:T(8,128)S(1)}, u32[]{:S(2)}, u32[]{:S(2)}) %collective-permute-start.4) | collective-permute-done | bytes 786464 | tf_op jit(solution)/shard_map/ppermute | solution.py:79
  183.4 6.4 %gather_fusion.1 = f32[8,64,6,512]{3,1,2,0:T(8,128)} fusion(f32[8,64,6,512]{3,1,2,0:T(8,128)} %bitcast.30, s32[1024]{0:T(1024)S(1)} %pad_clamp_fusion.1), kind=kCustom, calls=%fused_computation.1 | custom fusion | bytes 12582944 | tf_op jit(solution)/shard_map/gather | solution.py:80
  189.8 5.6 %gather_fusion.2 = f32[32,64,512]{2,1,0:T(8,128)} fusion(f32[64,48,512]{2,0,1:T(8,128)} %bitcast.116, s32[1024]{0:T(1024)S(1)} %get-tuple-element.20), kind=kCustom, calls=%fused_computation.2 | custom fusion | bytes 8388736 | tf_op jit(solution)/shard_map/jit(_take)/gather | solution.py:84
  195.4 5.0 %fusion = f32[64,32,1,512]{3,0,2,1:T(8,128)} fusion(f32[32,64,512]{2,1,0:T(8,128)} %gather_fusion.2, pred[32]{0:T(512)(128)(4,1)S(1)} %get-tuple-element.9), kind=kLoop, calls=%fused_computation.5 | loop fusion | flops 1048576 | bytes 8388640 | tf_op jit(solution)/shard_map/jit(_take)/select_n | solution.py:84
  200.4 10.1 %all-to-all-start.2 = ((f32[64,32,1,512]{3,0,2,1:T(8,128)}), f32[64,32,1,512]{3,0,2,1:T(8,128)}, u32[]{:S(2)}, u32[]{:S(2)}) async-start(f32[64,32,1,512]{3,0,2,1:T(8,128)} %fusion), calls=%async_computation.2 | async-start | bytes 8388608 | tf_op jit(solution)/shard_map/all_to_all | solution.py:115
  224.1 7.0 %fusion.8 = f32[512,512]{1,0:T(8,128)S(1)} fusion(f32[32,64,1,512]{3,0,1,2:T(8,128)S(1)} %copy_dynamic-update-slice_fusion, f32[1,2,512,512]{3,2,1,0:T(8,128)S(1)} %broadcast_subtract_fusion), kind=kOutput, calls=%fused_computation.16 | convolution fusion | flops 6442713088 | bytes 6291456 | tf_op jit(solution)/shard_map/qda,qdb->dab/dot_general | solution.py:112
  231.2 8.3 %fusion.24 = f32[2048,512]{1,0:T(8,128)} fusion(f32[2048,512]{1,0:T(8,128)S(1)} %bitcast.112, f32[512,512]{1,0:T(8,128)S(1)} %fusion.8), kind=kOutput, calls=%fused_computation.73 | convolution fusion | flops 6442450944 | bytes 9437184 | tf_op jit(solution)/shard_map/dab,qdb->qda/dot_general | solution.py:114
  239.5 68.4 %all-to-all-done.2 = f32[64,32,1,512]{3,0,2,1:T(8,128)} async-done(((f32[64,32,1,512]{3,0,2,1:T(8,128)}), f32[64,32,1,512]{3,0,2,1:T(8,128)}, u32[]{:S(2)}, u32[]{:S(2)}) %all-to-all-start.2) | async-done | bytes 4194336 | tf_op jit(solution)/shard_map/all_to_all | solution.py:115
  307.9 9.9 %fusion.12 = f32[512,512]{1,0:T(8,128)S(1)} fusion(f32[2048,512]{1,0:T(8,128)} %bitcast.42, f32[2048,512]{1,0:T(8,128)} %bitcast.113, f32[1,2,512,512]{3,2,1,0:T(8,128)} %copy-done.5), kind=kOutput, calls=%fused_computation.18 | convolution fusion | flops 6442713088 | bytes 10485760 | tf_op jit(solution)/shard_map/qda,qdkb->dkab/dot_general | solution.py:116
  317.8 8.6 %add_bitcast_fusion = f32[2048,1,512]{2,0,1:T(8,128)S(1)} fusion(f32[2048,512]{1,0:T(8,128)S(1)} %copy-done.4, f32[2048,512]{1,0:T(8,128)} %bitcast.42, f32[512,512]{1,0:T(8,128)S(1)} %fusion.12), kind=kOutput, calls=%fused_computation.9 | convolution fusion | flops 6443499520 | bytes 13631488 | tf_op jit(solution)/shard_map/dkab,qdkb->qda/dot_general | solution.py:118
  326.3 8.0 %copy.31 = f32[2048,1,512]{2,1,0:T(1,128)S(1)} copy(f32[2048,1,512]{2,0,1:T(8,128)S(1)} %add_bitcast_fusion) | data formatting | bytes 8388608 | tf_op jit(solution)/shard_map/add | solution.py:118
  334.3 100.0 %all_to_all.43 = f32[2048,1,512]{2,1,0:T(1,128)S(1)} all-to-all(f32[2048,1,512]{2,1,0:T(1,128)S(1)} %copy.31), channel_id=1, replica_groups=mesh['aux'=32,'occ'=8] {'aux'}, dimensions={0} | all-to-all | bytes 8388608 | tf_op jit(solution)/shard_map/all_to_all | solution.py:121
  434.3 4.4 %copy.37 = f32[32,64,1,512]{3,0,1,2:T(8,128)} copy(f32[32,64,1,512]{3,2,1,0:T(1,128)S(1)} %bitcast.117) | data formatting | bytes 8388608 | tf_op jit(solution)/shard_map/all_to_all | solution.py:121
  (68 shorter events, 42.6 us)
Async XLA Ops:
  0.0 1.4 copy-start
  13.7 2.7 copy-start.3
  16.4 14.2 %copy-start.7 = (s32[256,1]{0,1:T(1,128)S(1)}, s32[256,1]{0,1:T(1,128)}, u32[]{:S(2)}) copy-start(s32[256,1]{0,1:T(1,128)} %param.9) | copy-start | bytes 3076
  18.9 61.0 %all-to-all-start = ((f32[32,32,1,512]{3,1,2,0:T(8,128)}), f32[32,32,1,512]{3,1,2,0:T(8,128)}, u32[]{:S(2)}, u32[]{:S(2)}) async-start(f32[32,32,1,512]{3,1,2,0:T(8,128)} %copy.20), calls=%async_computation | async-start | bytes 4194304 | tf_op jit(solution)/shard_map/all_to_all | solution.py:43
  79.9 120.4 %all-to-all-start.1 = ((f32[32,32,1,512]{3,1,2,0:T(8,128)}), f32[32,32,1,512]{3,1,2,0:T(8,128)}, u32[]{:S(2)}, u32[]{:S(2)}) async-start(f32[32,32,1,512]{3,1,2,0:T(8,128)} %copy.21), calls=%async_computation.1 | async-start | bytes 4194304 | tf_op jit(solution)/shard_map/all_to_all | solution.py:43
  104.9 6.2 %collective-permute-start = (f32[64,1,6,512]{3,0,2,1:T(8,128)S(1)}, f32[64,1,6,512]{3,0,2,1:T(8,128)S(1)}, u32[]{:S(2)}, u32[]{:S(2)}) collective-permute-start(f32[64,1,6,512]{3,0,2,1:T(8,128)S(1)} %get-tuple-element.17), channel_id=1, source_target_pairs={{0,1},{1,0},{2,3},{3,2},{4,5},{5,4},{6,7},{7,6},{8,9},{9,8},{10,11... | collective-permute-start | bytes 2359304 | tf_op jit(solution)/shard_map/ppermute | solution.py:79
  105.0 20.4 %collective-permute-start.1 = (f32[64,1,6,512]{3,0,2,1:T(8,128)S(1)}, f32[64,1,6,512]{3,0,2,1:T(8,128)S(1)}, u32[]{:S(2)}, u32[]{:S(2)}) collective-permute-start(f32[64,1,6,512]{3,0,2,1:T(8,128)S(1)} %get-tuple-element.16), channel_id=1, source_target_pairs={{0,2},{1,3},{2,0},{3,1},{4,6},{5,7},{6,4},{7,5},{8,10},{9,11},{10,... | collective-permute-start | bytes 2359304 | tf_op jit(solution)/shard_map/ppermute | solution.py:79
  106.7 34.7 %collective-permute-start.2 = (f32[64,1,6,512]{3,0,2,1:T(8,128)S(1)}, f32[64,1,6,512]{3,0,2,1:T(8,128)S(1)}, u32[]{:S(2)}, u32[]{:S(2)}) collective-permute-start(f32[64,1,6,512]{3,0,2,1:T(8,128)S(1)} %get-tuple-element.15), channel_id=1, source_target_pairs={{0,3},{1,2},{2,1},{3,0},{4,7},{5,6},{6,5},{7,4},{8,11},{9,10},{10,... | collective-permute-start | bytes 2359304 | tf_op jit(solution)/shard_map/ppermute | solution.py:79
  106.9 54.8 %collective-permute-start.3 = (f32[64,1,6,512]{3,0,2,1:T(8,128)S(1)}, f32[64,1,6,512]{3,0,2,1:T(8,128)S(1)}, u32[]{:S(2)}, u32[]{:S(2)}) collective-permute-start(f32[64,1,6,512]{3,0,2,1:T(8,128)S(1)} %get-tuple-element.14), channel_id=1, source_target_pairs={{0,4},{1,5},{2,6},{3,7},{4,0},{5,1},{6,2},{7,3},{8,12},{9,13},{10,... | collective-permute-start | bytes 2359304 | tf_op jit(solution)/shard_map/ppermute | solution.py:79
  110.1 67.5 %collective-permute-start.4 = (f32[64,1,6,512]{3,0,2,1:T(8,128)S(1)}, f32[64,1,6,512]{3,0,2,1:T(8,128)S(1)}, u32[]{:S(2)}, u32[]{:S(2)}) collective-permute-start(f32[64,1,6,512]{3,0,2,1:T(8,128)S(1)} %get-tuple-element.13), channel_id=1, source_target_pairs={{0,5},{1,4},{2,7},{3,6},{4,1},{5,0},{6,3},{7,2},{8,13},{9,12},{10,... | collective-permute-start | bytes 2359304 | tf_op jit(solution)/shard_map/ppermute | solution.py:79
  111.1 67.5 %collective-permute-start.5 = (f32[64,1,6,512]{3,0,2,1:T(8,128)S(1)}, f32[64,1,6,512]{3,0,2,1:T(8,128)S(1)}, u32[]{:S(2)}, u32[]{:S(2)}) collective-permute-start(f32[64,1,6,512]{3,0,2,1:T(8,128)S(1)} %get-tuple-element.12), channel_id=1, source_target_pairs={{0,6},{1,7},{2,4},{3,5},{4,2},{5,3},{6,0},{7,1},{8,14},{9,15},{10,... | collective-permute-start | bytes 2359304 | tf_op jit(solution)/shard_map/ppermute | solution.py:79
  125.4 57.0 %collective-permute-start.6 = (f32[64,1,6,512]{3,0,2,1:T(8,128)S(1)}, f32[64,1,6,512]{3,0,2,1:T(8,128)S(1)}, u32[]{:S(2)}, u32[]{:S(2)}) collective-permute-start(f32[64,1,6,512]{3,0,2,1:T(8,128)S(1)} %get-tuple-element.11), channel_id=1, source_target_pairs={{0,7},{1,6},{2,5},{3,4},{4,3},{5,2},{6,1},{7,0},{8,15},{9,14},{10,... | collective-permute-start | bytes 2359304 | tf_op jit(solution)/shard_map/ppermute | solution.py:79
  200.3 10.8 %copy-start.8 = (f32[256]{0:T(256)S(1)}, f32[256]{0:T(256)}, u32[]{:S(2)}) copy-start(f32[256]{0:T(256)} %param.7) | copy-start | bytes 3076
  200.4 14.5 %copy-start.6 = (f32[512]{0:T(512)S(1)}, f32[512]{0:T(512)}, u32[]{:S(2)}) copy-start(f32[512]{0:T(512)} %param.8) | copy-start | bytes 6148
  200.4 107.5 %all-to-all-start.2 = ((f32[64,32,1,512]{3,0,2,1:T(8,128)}), f32[64,32,1,512]{3,0,2,1:T(8,128)}, u32[]{:S(2)}, u32[]{:S(2)}) async-start(f32[64,32,1,512]{3,0,2,1:T(8,128)} %fusion), calls=%async_computation.2 | async-start | bytes 8388608 | tf_op jit(solution)/shard_map/all_to_all | solution.py:115
  215.3 8.8 %copy-start.5 = (f32[1,2,512,512]{3,2,1,0:T(8,128)}, f32[1,2,512,512]{3,2,1,0:T(8,128)S(1)}, u32[]{:S(2)}) copy-start(f32[1,2,512,512]{3,2,1,0:T(8,128)S(1)} %broadcast_subtract_fusion) | copy-start | bytes 6291460
  224.1 7.0 %copy-start.2 = (f32[32,64,1,512]{3,1,0,2:T(8,128)}, f32[32,64,1,512]{3,1,0,2:T(8,128)S(1)}, u32[]{:S(2)}) copy-start(f32[32,64,1,512]{3,1,0,2:T(8,128)S(1)} %copy.24) | copy-start | bytes 12582916
  307.9 9.9 %copy-start.4 = (f32[2048,512]{1,0:T(8,128)S(1)}, f32[2048,512]{1,0:T(8,128)}, u32[]{:S(2)}) copy-start(f32[2048,512]{1,0:T(8,128)} %fusion.24) | copy-start | bytes 12582916
  434.3 4.4 %copy-start.1 = (f32[768,512]{1,0:T(8,128)S(1)}, f32[768,512]{1,0:T(8,128)}, u32[]{:S(2)}) copy-start(f32[768,512]{1,0:T(8,128)} %param.6) | copy-start | bytes 4718596
